TPU v7x, 32 devices: a whole 2x2x4 slice. The times are simulated.
32 devices in a mesh: nodes: 8 (over z, x), mp: 4 (over y, core).
Axes of the slice: x: 2, y: 2, z: 4, core: 2. Of those that a mesh axis runs over, the one named last changes fastest.
Arguments:
- grid_in: bfloat16 [8192, 1024], P('nodes', 'mp'), may hold values from -2200 to 2200
- mesh_in: bfloat16 [2048, 1024], P('nodes', 'mp'), may hold values from -2200 to 2200
- w_query: bfloat16 [4, 1024, 512], P(None, None, 'mp'), as said below
- w_key: bfloat16 [4, 1024, 512], P(None, None, 'mp'), may hold values from -8 to 8
- w_value: bfloat16 [4, 1024, 512], P(None, None, 'mp'), may hold values from -0.1875 to 0.1875
- w_out: bfloat16 [4, 512, 1024], P(None, 'mp'), may hold values from -1 to 1
- norm_gains: float32 [6, 1024], replicated, may hold values from 0.25 to 1.75
- enc_list: int32 [16, 4], P('nodes'), may hold values from 0 to 63, as said below
- proc_list: int32 [16, 3], P('nodes'), may hold values from 0 to 15, as said below
- dec_list: int32 [64, 2], P('nodes'), may hold values from 0 to 15, as said below
- grid_count: int32 [64], replicated, may hold values from 1 to 128
Outputs:
- grid_out: bfloat16 [8192, 1024], P('nodes', 'mp')
- mesh_out: bfloat16 [2048, 1024], P('nodes', 'mp')
Inputs may be any that keep to these rules, and one draw needn't show every extreme that they name: `enc_list`: mesh block b lies with node index b // 2; its 4 entries are distinct grid blocks held by node indices at most 2 from it (grid block c lies with node index c // 8). `proc_list`: entry 0 of row b is b; the others are distinct mesh blocks other than b held by node indices at most 2 from b's. `dec_list`: grid block c's 2 entries are distinct mesh blocks held by node indices at most 2 from c's. `w_query`: entries within 6 / sqrt(1024) of zero.
All inputs are finite; a program needn't handle non-finite values.
Results may differ from a plain program's by a relative error of at most 0.019.
Values may be sent and summed in bfloat16 or wider, within the bound.
A program may use at most 64 MiB of HBM per device.

v0:
```python
import jax
import jax.numpy as jnp
from jax import lax
from jax.sharding import PartitionSpec as P

HEAD_DIM = 64
BLOCK = 128
REACH = 2


epsilon = 1e-05


def from_behind(value, axis, steps):
    count = lax.axis_size(axis)
    first, last = (max(0, -steps), min(count, count - steps))
    return lax.ppermute(value, axis, [(source, source + steps) for source in range(first, last)])


def normalize(states, gains):
    values = states.astype(jnp.float32)
    average = jnp.mean(values, axis=-1, keepdims=True)
    centred = values - average
    spread = jnp.mean(centred * centred, axis=-1, keepdims=True)
    return (centred * lax.rsqrt(spread + epsilon) * gains).astype(jnp.bfloat16)


def project(inputs, weight):
    return jnp.dot(inputs, weight, preferred_element_type=jnp.float32).astype(jnp.bfloat16)


def attend(queries, key_rows, values, key_ok):
    batch_count, row_count, head_width = queries.shape
    key_count = key_rows.shape[1]
    head_count = head_width // HEAD_DIM
    query_heads = queries.reshape(batch_count, row_count, head_count, HEAD_DIM)
    key_heads = key_rows.reshape(batch_count, key_count, head_count, HEAD_DIM)
    value_heads = values.reshape(batch_count, key_count, head_count, HEAD_DIM)
    scores = jnp.einsum(
        "brhd,bkhd->bhrk", query_heads, key_heads, preferred_element_type=jnp.float32
    ) * HEAD_DIM ** (-0.5)
    if key_ok is not None:
        scores = jnp.where(key_ok[:, None, None, :], scores, -1e30)
    highest = jnp.max(scores, axis=-1, keepdims=True)
    weights = jnp.exp(scores - highest)
    chances = (weights / jnp.sum(weights, axis=-1, keepdims=True)).astype(jnp.bfloat16)
    blended = jnp.einsum(
        "bhrk,bkhd->brhd", chances, value_heads, preferred_element_type=jnp.float32
    )
    return blended.astype(jnp.bfloat16).reshape(batch_count * row_count, head_width)


def window(inputs, fetch):
    pieces = []
    for offset in range(-REACH, REACH + 1):
        pieces.append(inputs if offset == 0 else fetch(inputs, offset))
    return jnp.concatenate(pieces, axis=0)


def pick(beside_all, listed, window_start):
    blocks = beside_all.reshape(-1, BLOCK, beside_all.shape[1])
    local_ids = listed - window_start
    chosen = jnp.take(blocks, local_ids, axis=0)
    return chosen.reshape(listed.shape[0], listed.shape[1] * BLOCK, beside_all.shape[1])


def by_groups(every_head, columns, head_width):
    summed = jnp.zeros((every_head.shape[0], columns.shape[1]), jnp.float32)
    for member in range(columns.shape[0] // head_width):
        piece = jnp.dot(
            every_head[:, member * head_width : (member + 1) * head_width],
            columns[member * head_width : (member + 1) * head_width],
            preferred_element_type=jnp.float32,
        ).astype(jnp.bfloat16)
        piece = lax.optimization_barrier(piece)
        summed = summed + piece.astype(jnp.float32)
    return summed


def keys_values(normed, key_weight, value_weight):
    return jnp.concatenate([project(normed, key_weight), project(normed, value_weight)], axis=1)


def listed_valid(listed, grid_count):
    every_block = jnp.arange(grid_count.shape[0])
    counts = jnp.sum(
        jnp.where(listed[:, :, None] == every_block[None, None, :], grid_count[None, None, :], 0),
        axis=-1,
    )
    return jnp.arange(BLOCK)[None, None, :] < counts[:, :, None]


def per_device(
    grid_in,
    mesh_in,
    w_query,
    w_key,
    w_value,
    w_out,
    norm_gains,
    enc_list,
    proc_list,
    dec_list,
    grid_count,
):
    node_index = lax.axis_index("nodes")
    head_width = w_query.shape[2]
    grid_blocks = grid_in.shape[0] // BLOCK
    mesh_blocks = mesh_in.shape[0] // BLOCK
    grid_full, mesh_full = (
        lax.all_gather(grid_in, "mp", axis=1, tiled=True),
        lax.all_gather(mesh_in, "mp", axis=1, tiled=True),
    )
    out_columns = lax.all_to_all(w_out, "mp", split_axis=2, concat_axis=1, tiled=True)
    own_counts = lax.dynamic_slice_in_dim(grid_count, node_index * grid_blocks, grid_blocks)
    row_ok = (jnp.arange(BLOCK)[None, :] < own_counts[:, None]).reshape(-1, 1)

    def mesh_update(blended, layer_index, state_part):
        whole_new = None
        every_head = lax.all_gather(blended, "mp", axis=1, tiled=True)
        update = by_groups(every_head, out_columns[layer_index], head_width)
        part_new = (state_part.astype(jnp.float32) + update).astype(jnp.bfloat16)
        whole_new = lax.all_gather(part_new, "mp", axis=1, tiled=True)
        return (part_new, whole_new)

    mesh_queries = project(normalize(mesh_full, norm_gains[0]), w_query[0]).reshape(
        mesh_blocks, BLOCK, head_width
    )
    grid_normed = normalize(grid_full, norm_gains[1])
    grid_kv = keys_values(grid_normed, w_key[0], w_value[0])
    listed_ok = listed_valid(enc_list, grid_count).reshape(enc_list.shape[0], -1)
    beside_all = window(grid_kv, lambda inputs, offset: from_behind(inputs, "nodes", -offset))
    chosen = pick(beside_all, enc_list, (node_index - REACH) * grid_blocks)
    blended = attend(mesh_queries, chosen[:, :, :head_width], chosen[:, :, head_width:], listed_ok)
    state_part, state_whole = mesh_update(blended, 0, mesh_in)
    for layer_index in (1, 2):
        normed = normalize(state_whole, norm_gains[layer_index + 1])
        queries = project(normed, w_query[layer_index]).reshape(mesh_blocks, BLOCK, head_width)
        mesh_kv = keys_values(normed, w_key[layer_index], w_value[layer_index])
        beside_all = window(mesh_kv, lambda inputs, offset: from_behind(inputs, "nodes", -offset))
        chosen = pick(beside_all, proc_list, (node_index - REACH) * mesh_blocks)
        blended = attend(queries, chosen[:, :, :head_width], chosen[:, :, head_width:], None)
        state_part, state_whole = mesh_update(blended, layer_index, state_part)
    grid_queries = project(normalize(grid_full, norm_gains[4]), w_query[3]).reshape(
        grid_blocks, BLOCK, head_width
    )
    mesh_normed = normalize(state_whole, norm_gains[5])
    mesh_kv = keys_values(mesh_normed, w_key[3], w_value[3])
    beside_all = window(mesh_kv, lambda inputs, offset: from_behind(inputs, "nodes", -offset))
    chosen = pick(beside_all, dec_list, (node_index - REACH) * mesh_blocks)
    blended = attend(grid_queries, chosen[:, :, :head_width], chosen[:, :, head_width:], None)
    every_head = lax.all_gather(blended, "mp", axis=1, tiled=True)
    update = by_groups(every_head, out_columns[3], head_width)
    grid_out = grid_in.astype(jnp.float32) + update
    grid_out = jnp.where(row_ok, grid_out, 0.0).astype(jnp.bfloat16)
    return (grid_out, state_part)


def solution(mesh):
    placed = (
        P("nodes", "mp"),
        P("nodes", "mp"),
        P(None, None, "mp"),
        P(None, None, "mp"),
        P(None, None, "mp"),
        P(None, "mp", None),
        P(),
        P("nodes", None),
        P("nodes", None),
        P("nodes", None),
        P(),
    )
    return jax.shard_map(
        per_device,
        mesh=mesh,
        in_specs=placed,
        out_specs=(P("nodes", "mp"), P("nodes", "mp")),
        check_vma=False,
    )
```

profile of v0, /device:TPU:11, one launch (start us, length us, event | category | flops | bytes accessed | tf_op | source)
XLA Modules:
  0.0 291.1 jit_solution(6728711550272002024)
XLA Ops:
  10.4 4.9 %all-to-all-start = ((bf16[4,128,1024]{1,0,2:T(4,128)(2,1)}), bf16[4,128,1024]{1,0,2:T(4,128)(2,1)}, u32[]{:S(2)}, u32[]{:S(2)}) async-start(bf16[4,128,1024]{1,0,2:T(4,128)(2,1)} %copy.131), calls=%async_computation | async-start | bytes 2097152 | tf_op jit(solution)/shard_map/all_to_all | solution.py:114
  15.5 28.9 %all_gather.28 = bf16[256,1024]{1,0:T(8,128)(2,1)S(1)} all-gather(bf16[256,256]{1,0:T(8,128)(2,1)S(1)} %copy-done.9), channel_id=1, replica_groups=mesh['nodes'=8,'mp'=4] {'mp'}, dimensions={1}, use_global_device_ids=true | all-gather | bytes 655360 | tf_op jit(solution)/shard_map/all_gather | solution.py:112
  56.3 3.2 %collective-permute-start = (bf16[1024,256]{0,1:T(8,128)(2,1)}, bf16[1024,256]{0,1:T(8,128)(2,1)}, u32[]{:S(2)}, u32[]{:S(2)}) collective-permute-start(bf16[1024,256]{0,1:T(8,128)(2,1)} %pad_maximum_fusion), channel_id=1, source_target_pairs={{0,8},{4,12},{8,16},{12,20},{16,24},{20,28},{1,9},{5,13},{9,17},{1... | collective-permute-start | bytes 1572872 | tf_op jit(solution)/shard_map/ppermute | solution.py:17
  60.4 3.2 %collective-permute-start.1 = (bf16[1024,256]{0,1:T(8,128)(2,1)}, bf16[1024,256]{0,1:T(8,128)(2,1)}, u32[]{:S(2)}, u32[]{:S(2)}) collective-permute-start(bf16[1024,256]{0,1:T(8,128)(2,1)} %pad_maximum_fusion), channel_id=1, source_target_pairs={{0,4},{4,8},{8,12},{12,16},{16,20},{20,24},{24,28},{1,5},{5,9},{9,... | collective-permute-start | bytes 1572872 | tf_op jit(solution)/shard_map/ppermute | solution.py:17
  66.4 3.7 %collective-permute-start.3 = (bf16[1024,256]{0,1:T(8,128)(2,1)}, bf16[1024,256]{0,1:T(8,128)(2,1)}, u32[]{:S(2)}, u32[]{:S(2)}) collective-permute-start(bf16[1024,256]{0,1:T(8,128)(2,1)} %pad_maximum_fusion), channel_id=1, source_target_pairs={{8,0},{12,4},{16,8},{20,12},{24,16},{28,20},{9,1},{13,5},{17,9},{2... | collective-permute-start | bytes 1572872 | tf_op jit(solution)/shard_map/ppermute | solution.py:17
  75.4 11.5 %collective-permute-done.1 = bf16[1024,256]{0,1:T(8,128)(2,1)} collective-permute-done((bf16[1024,256]{0,1:T(8,128)(2,1)}, bf16[1024,256]{0,1:T(8,128)(2,1)}, u32[]{:S(2)}, u32[]{:S(2)}) %collective-permute-start.1) | collective-permute-done | bytes 524320 | tf_op jit(solution)/shard_map/ppermute | solution.py:17
  93.5 4.4 %copy.167 = bf16[5120,256]{1,0:T(8,128)(2,1)} copy(bf16[5120,256]{0,1:T(8,128)(2,1)} %constant_dynamic-update-slice_fusion) | data formatting | bytes 5242880 | tf_op jit(solution)/shard_map/reshape | solution.py:61
  97.9 3.2 %gather_fusion = bf16[8,128,256]{2,1,0:T(8,128)(2,1)} fusion(bf16[40,128,256]{2,1,0:T(8,128)(2,1)} %bitcast.219, s32[1024]{0:T(1024)} %pad_clamp_fusion.2), kind=kCustom, calls=%fused_computation.2 | custom fusion | bytes 1048608 | tf_op jit(solution)/shard_map/jit(_take)/gather | solution.py:63
  109.1 2.7 fusion.36
  111.9 6.9 %all_gather.29 = bf16[256,512]{0,1:T(8,128)(2,1)S(1)} all-gather(bf16[256,128]{0,1:T(8,128)(2,1)S(1)} %bitcast.238), channel_id=1, replica_groups=mesh['nodes'=8,'mp'=4] {'mp'}, dimensions={1}, use_global_device_ids=true | all-gather | bytes 327680 | tf_op jit(solution)/shard_map/all_gather | solution.py:120
  119.8 7.3 %all_gather.30 = bf16[256,1024]{1,0:T(8,128)(2,1)S(1)} all-gather(bf16[256,256]{1,0:T(8,128)(2,1)S(1)} %add_convert_fusion.2), channel_id=1, replica_groups=mesh['nodes'=8,'mp'=4] {'mp'}, dimensions={1}, use_global_device_ids=true | all-gather | bytes 655360 | tf_op jit(solution)/shard_map/all_gather | solution.py:123
  130.4 3.2 %collective-permute-start.4 = (bf16[256,256]{0,1:T(8,128)(2,1)S(1)}, bf16[256,256]{0,1:T(8,128)(2,1)}, u32[]{:S(2)}, u32[]{:S(2)}) collective-permute-start(bf16[256,256]{0,1:T(8,128)(2,1)S(1)} %pad_maximum_fusion.1), channel_id=1, source_target_pairs={{0,8},{4,12},{8,16},{12,20},{16,24},{20,28},{1,9},{5,13},{9,17},{1... | collective-permute-start | bytes 393224 | tf_op jit(solution)/shard_map/ppermute | solution.py:17
  136.0 3.0 %collective-permute-start.6 = (bf16[256,256]{0,1:T(8,128)(2,1)S(1)}, bf16[256,256]{0,1:T(8,128)(2,1)}, u32[]{:S(2)}, u32[]{:S(2)}) collective-permute-start(bf16[256,256]{0,1:T(8,128)(2,1)S(1)} %pad_maximum_fusion.1), channel_id=1, source_target_pairs={{4,0},{8,4},{12,8},{16,12},{20,16},{24,20},{28,24},{5,1},{9,5},{13... | collective-permute-start | bytes 393224 | tf_op jit(solution)/shard_map/ppermute | solution.py:17
  139.0 3.5 %collective-permute-start.7 = (bf16[256,256]{0,1:T(8,128)(2,1)S(1)}, bf16[256,256]{0,1:T(8,128)(2,1)S(1)}, u32[]{:S(2)}, u32[]{:S(2)}) collective-permute-start(bf16[256,256]{0,1:T(8,128)(2,1)S(1)} %pad_maximum_fusion.1), channel_id=1, source_target_pairs={{8,0},{12,4},{16,8},{20,12},{24,16},{28,20},{9,1},{13,5},{17,9},{2... | collective-permute-start | bytes 393224 | tf_op jit(solution)/shard_map/ppermute | solution.py:17
  164.4 6.9 %all_gather.31 = bf16[256,512]{0,1:T(8,128)(2,1)S(1)} all-gather(bf16[256,128]{0,1:T(8,128)(2,1)S(1)} %bitcast.239), channel_id=1, replica_groups=mesh['nodes'=8,'mp'=4] {'mp'}, dimensions={1}, use_global_device_ids=true | all-gather | bytes 327680 | tf_op jit(solution)/shard_map/all_gather | solution.py:120
  172.3 7.3 %all_gather.32 = bf16[256,1024]{1,0:T(8,128)(2,1)S(1)} all-gather(bf16[256,256]{1,0:T(8,128)(2,1)S(1)} %add_convert_fusion.1), channel_id=1, replica_groups=mesh['nodes'=8,'mp'=4] {'mp'}, dimensions={1}, use_global_device_ids=true | all-gather | bytes 655360 | tf_op jit(solution)/shard_map/all_gather | solution.py:123
  184.8 3.2 %collective-permute-start.9 = (bf16[256,256]{0,1:T(8,128)(2,1)S(1)}, bf16[256,256]{0,1:T(8,128)(2,1)}, u32[]{:S(2)}, u32[]{:S(2)}) collective-permute-start(bf16[256,256]{0,1:T(8,128)(2,1)S(1)} %pad_maximum_fusion.2), channel_id=1, source_target_pairs={{0,4},{4,8},{8,12},{12,16},{16,20},{20,24},{24,28},{1,5},{5,9},{9,... | collective-permute-start | bytes 393224 | tf_op jit(solution)/shard_map/ppermute | solution.py:17
  190.3 4.5 %collective-permute-start.11 = (bf16[256,256]{0,1:T(8,128)(2,1)S(1)}, bf16[256,256]{0,1:T(8,128)(2,1)S(1)}, u32[]{:S(2)}, u32[]{:S(2)}) collective-permute-start(bf16[256,256]{0,1:T(8,128)(2,1)S(1)} %pad_maximum_fusion.2), channel_id=1, source_target_pairs={{8,0},{12,4},{16,8},{20,12},{24,16},{28,20},{9,1},{13,5},{17,9},{2... | collective-permute-start | bytes 393224 | tf_op jit(solution)/shard_map/ppermute | solution.py:17
  215.5 6.9 %all_gather.33 = bf16[256,512]{0,1:T(8,128)(2,1)S(1)} all-gather(bf16[256,128]{0,1:T(8,128)(2,1)S(1)} %bitcast.240), channel_id=1, replica_groups=mesh['nodes'=8,'mp'=4] {'mp'}, dimensions={1}, use_global_device_ids=true | all-gather | bytes 327680 | tf_op jit(solution)/shard_map/all_gather | solution.py:120
  223.4 7.4 %all_gather.34 = bf16[256,1024]{1,0:T(8,128)(2,1)S(1)} all-gather(bf16[256,256]{1,0:T(8,128)(2,1)S(1)} %add_convert_fusion), channel_id=1, replica_groups=mesh['nodes'=8,'mp'=4] {'mp'}, dimensions={1}, use_global_device_ids=true | all-gather | bytes 655360 | tf_op jit(solution)/shard_map/all_gather | solution.py:123
  235.9 2.9 collective-permute-start.13
  245.7 4.9 %collective-permute-start.15 = (bf16[256,256]{0,1:T(8,128)(2,1)S(1)}, bf16[256,256]{0,1:T(8,128)(2,1)S(1)}, u32[]{:S(2)}, u32[]{:S(2)}) collective-permute-start(bf16[256,256]{0,1:T(8,128)(2,1)S(1)} %pad_maximum_fusion.3), channel_id=1, source_target_pairs={{8,0},{12,4},{16,8},{20,12},{24,16},{28,20},{9,1},{13,5},{17,9},{2... | collective-permute-start | bytes 393224 | tf_op jit(solution)/shard_map/ppermute | solution.py:17
  255.9 3.7 %fusion.35 = bf16[8,128,2,64]{1,3,2,0:T(8,128)(2,1)S(1)} fusion(bf16[8,256,2,64]{1,3,2,0:T(8,128)(2,1)S(1)} %bitcast.237, f32[8,2,128]{2,1,0:T(2,128)S(1)} %fusion.149, bf16[8,256,2,64]{1,3,2,0:T(8,128)(2,1)S(1)} %bitcast.236, bf16[8,128,2,64]{3,2,1,0:T(2,128)(2,1)S(1)} %copy-done.8), kind=kOutput, calls=%fused_computation.59 | convolution fusion | flops 136448256 | bytes 1581056 | tf_op jit(solution)/shard_map/bhrk,bkhd->brhd/dot_general | solution.py:47
  260.8 17.2 %all-gather.5.cloned.1.call-done = bf16[1024,512]{0,1:T(8,128)(2,1)} async-done(((bf16[1024,128]{0,1:T(8,128)(2,1)}), bf16[1024,512]{0,1:T(8,128)(2,1)}) %all-gather.5.cloned.1.call-update) | async-done | bytes 1048592 | tf_op jit(solution)/shard_map/all_gather | solution.py:152
  (218 shorter events, 121.6 us)
Async XLA Ops:
  7.2 41.0 %all-gather.3.cloned.1.call-start = ((), (), s32[]{:S(2)}) async-start(), calls=%async_computation.1 | async-start | bytes 2621440 | tf_op jit(solution)/shard_map/all_gather | solution.py:111
  7.9 37.0 %copy-start.21 = (s32[8,2]{0,1:T(2,128)S(1)}, s32[8,2]{0,1:T(2,128)}, u32[]{:S(2)}) copy-start(s32[8,2]{0,1:T(2,128)} %param.22) | copy-start | bytes 196
  7.9 37.0 %copy-start.22 = (s32[2,3]{1,0:T(2,128)S(1)}, s32[2,3]{1,0:T(2,128)}, u32[]{:S(2)}) copy-start(s32[2,3]{1,0:T(2,128)} %param.21) | copy-start | bytes 76
  8.0 38.3 %copy-start.11 = (f32[6,1024]{1,0:T(8,128)S(1)}, f32[6,1024]{1,0:T(8,128)}, u32[]{:S(2)}) copy-start(f32[6,1024]{1,0:T(8,128)} %param.19) | copy-start | bytes 73732
  10.4 61.7 %all-to-all-start = ((bf16[4,128,1024]{1,0,2:T(4,128)(2,1)}), bf16[4,128,1024]{1,0,2:T(4,128)(2,1)}, u32[]{:S(2)}, u32[]{:S(2)}) async-start(bf16[4,128,1024]{1,0,2:T(4,128)(2,1)} %copy.131), calls=%async_computation | async-start | bytes 2097152 | tf_op jit(solution)/shard_map/all_to_all | solution.py:114
  15.3 262.7 %all-gather.5.cloned.1.call-start = ((), (), s32[]{:S(2)}) async-start(), calls=%async_computation.2 | async-start | bytes 1310720 | tf_op jit(solution)/shard_map/all_gather | solution.py:152
  56.3 17.2 %collective-permute-start = (bf16[1024,256]{0,1:T(8,128)(2,1)}, bf16[1024,256]{0,1:T(8,128)(2,1)}, u32[]{:S(2)}, u32[]{:S(2)}) collective-permute-start(bf16[1024,256]{0,1:T(8,128)(2,1)} %pad_maximum_fusion), channel_id=1, source_target_pairs={{0,8},{4,12},{8,16},{12,20},{16,24},{20,28},{1,9},{5,13},{9,17},{1... | collective-permute-start | bytes 1572872 | tf_op jit(solution)/shard_map/ppermute | solution.py:17
  60.4 26.5 %collective-permute-start.1 = (bf16[1024,256]{0,1:T(8,128)(2,1)}, bf16[1024,256]{0,1:T(8,128)(2,1)}, u32[]{:S(2)}, u32[]{:S(2)}) collective-permute-start(bf16[1024,256]{0,1:T(8,128)(2,1)} %pad_maximum_fusion), channel_id=1, source_target_pairs={{0,4},{4,8},{8,12},{12,16},{16,20},{20,24},{24,28},{1,5},{5,9},{9,... | collective-permute-start | bytes 1572872 | tf_op jit(solution)/shard_map/ppermute | solution.py:17
  63.7 26.0 %collective-permute-start.2 = (bf16[1024,256]{0,1:T(8,128)(2,1)}, bf16[1024,256]{0,1:T(8,128)(2,1)}, u32[]{:S(2)}, u32[]{:S(2)}) collective-permute-start(bf16[1024,256]{0,1:T(8,128)(2,1)} %pad_maximum_fusion), channel_id=1, source_target_pairs={{4,0},{8,4},{12,8},{16,12},{20,16},{24,20},{28,24},{5,1},{9,5},{13... | collective-permute-start | bytes 1572872 | tf_op jit(solution)/shard_map/ppermute | solution.py:17
  66.4 25.1 %collective-permute-start.3 = (bf16[1024,256]{0,1:T(8,128)(2,1)}, bf16[1024,256]{0,1:T(8,128)(2,1)}, u32[]{:S(2)}, u32[]{:S(2)}) collective-permute-start(bf16[1024,256]{0,1:T(8,128)(2,1)} %pad_maximum_fusion), channel_id=1, source_target_pairs={{8,0},{12,4},{16,8},{20,12},{24,16},{28,20},{9,1},{13,5},{17,9},{2... | collective-permute-start | bytes 1572872 | tf_op jit(solution)/shard_map/ppermute | solution.py:17
  127.8 26.4 %copy-start.14 = (s32[1024]{0:T(1024)S(1)}, s32[1024]{0:T(1024)}, u32[]{:S(2)}) copy-start(s32[1024]{0:T(1024)} %get-tuple-element.24) | copy-start | bytes 12292
  130.4 15.5 %collective-permute-start.4 = (bf16[256,256]{0,1:T(8,128)(2,1)S(1)}, bf16[256,256]{0,1:T(8,128)(2,1)}, u32[]{:S(2)}, u32[]{:S(2)}) collective-permute-start(bf16[256,256]{0,1:T(8,128)(2,1)S(1)} %pad_maximum_fusion.1), channel_id=1, source_target_pairs={{0,8},{4,12},{8,16},{12,20},{16,24},{20,28},{1,9},{5,13},{9,17},{1... | collective-permute-start | bytes 393224 | tf_op jit(solution)/shard_map/ppermute | solution.py:17
  133.7 13.8 %collective-permute-start.5 = (bf16[256,256]{0,1:T(8,128)(2,1)S(1)}, bf16[256,256]{0,1:T(8,128)(2,1)}, u32[]{:S(2)}, u32[]{:S(2)}) collective-permute-start(bf16[256,256]{0,1:T(8,128)(2,1)S(1)} %pad_maximum_fusion.1), channel_id=1, source_target_pairs={{0,4},{4,8},{8,12},{12,16},{16,20},{20,24},{24,28},{1,5},{5,9},{9,... | collective-permute-start | bytes 393224 | tf_op jit(solution)/shard_map/ppermute | solution.py:17
  136.0 13.8 %collective-permute-start.6 = (bf16[256,256]{0,1:T(8,128)(2,1)S(1)}, bf16[256,256]{0,1:T(8,128)(2,1)}, u32[]{:S(2)}, u32[]{:S(2)}) collective-permute-start(bf16[256,256]{0,1:T(8,128)(2,1)S(1)} %pad_maximum_fusion.1), channel_id=1, source_target_pairs={{4,0},{8,4},{12,8},{16,12},{20,16},{24,20},{28,24},{5,1},{9,5},{13... | collective-permute-start | bytes 393224 | tf_op jit(solution)/shard_map/ppermute | solution.py:17
  139.0 12.4 %collective-permute-start.7 = (bf16[256,256]{0,1:T(8,128)(2,1)S(1)}, bf16[256,256]{0,1:T(8,128)(2,1)S(1)}, u32[]{:S(2)}, u32[]{:S(2)}) collective-permute-start(bf16[256,256]{0,1:T(8,128)(2,1)S(1)} %pad_maximum_fusion.1), channel_id=1, source_target_pairs={{8,0},{12,4},{16,8},{20,12},{24,16},{28,20},{9,1},{13,5},{17,9},{2... | collective-permute-start | bytes 393224 | tf_op jit(solution)/shard_map/ppermute | solution.py:17
  181.6 26.6 %copy-start.17 = (pred[2,3]{1,0:T(4,128)(4,1)S(1)}, pred[2,3]{1,0:T(4,128)(4,1)}, u32[]{:S(2)}) copy-start(pred[2,3]{1,0:T(4,128)(4,1)} %get-tuple-element.5) | copy-start | bytes 22
  182.9 15.3 %collective-permute-start.8 = (bf16[256,256]{0,1:T(8,128)(2,1)S(1)}, bf16[256,256]{0,1:T(8,128)(2,1)}, u32[]{:S(2)}, u32[]{:S(2)}) collective-permute-start(bf16[256,256]{0,1:T(8,128)(2,1)S(1)} %pad_maximum_fusion.2), channel_id=1, source_target_pairs={{0,8},{4,12},{8,16},{12,20},{16,24},{20,28},{1,9},{5,13},{9,17},{1... | collective-permute-start | bytes 393224 | tf_op jit(solution)/shard_map/ppermute | solution.py:17
  184.8 15.0 %collective-permute-start.9 = (bf16[256,256]{0,1:T(8,128)(2,1)S(1)}, bf16[256,256]{0,1:T(8,128)(2,1)}, u32[]{:S(2)}, u32[]{:S(2)}) collective-permute-start(bf16[256,256]{0,1:T(8,128)(2,1)S(1)} %pad_maximum_fusion.2), channel_id=1, source_target_pairs={{0,4},{4,8},{8,12},{12,16},{16,20},{20,24},{24,28},{1,5},{5,9},{9,... | collective-permute-start | bytes 393224 | tf_op jit(solution)/shard_map/ppermute | solution.py:17
  188.1 14.0 %collective-permute-start.10 = (bf16[256,256]{0,1:T(8,128)(2,1)S(1)}, bf16[256,256]{0,1:T(8,128)(2,1)}, u32[]{:S(2)}, u32[]{:S(2)}) collective-permute-start(bf16[256,256]{0,1:T(8,128)(2,1)S(1)} %pad_maximum_fusion.2), channel_id=1, source_target_pairs={{4,0},{8,4},{12,8},{16,12},{20,16},{24,20},{28,24},{5,1},{9,5},{13... | collective-permute-start | bytes 393224 | tf_op jit(solution)/shard_map/ppermute | solution.py:17
  190.3 13.4 %collective-permute-start.11 = (bf16[256,256]{0,1:T(8,128)(2,1)S(1)}, bf16[256,256]{0,1:T(8,128)(2,1)S(1)}, u32[]{:S(2)}, u32[]{:S(2)}) collective-permute-start(bf16[256,256]{0,1:T(8,128)(2,1)S(1)} %pad_maximum_fusion.2), channel_id=1, source_target_pairs={{8,0},{12,4},{16,8},{20,12},{24,16},{28,20},{9,1},{13,5},{17,9},{2... | collective-permute-start | bytes 393224 | tf_op jit(solution)/shard_map/ppermute | solution.py:17
  234.0 16.6 %collective-permute-start.12 = (bf16[256,256]{0,1:T(8,128)(2,1)S(1)}, bf16[256,256]{0,1:T(8,128)(2,1)}, u32[]{:S(2)}, u32[]{:S(2)}) collective-permute-start(bf16[256,256]{0,1:T(8,128)(2,1)S(1)} %pad_maximum_fusion.3), channel_id=1, source_target_pairs={{0,8},{4,12},{8,16},{12,20},{16,24},{20,28},{1,9},{5,13},{9,17},{1... | collective-permute-start | bytes 393224 | tf_op jit(solution)/shard_map/ppermute | solution.py:17
  235.9 15.6 %collective-permute-start.13 = (bf16[256,256]{0,1:T(8,128)(2,1)S(1)}, bf16[256,256]{0,1:T(8,128)(2,1)}, u32[]{:S(2)}, u32[]{:S(2)}) collective-permute-start(bf16[256,256]{0,1:T(8,128)(2,1)S(1)} %pad_maximum_fusion.3), channel_id=1, source_target_pairs={{0,4},{4,8},{8,12},{12,16},{16,20},{20,24},{24,28},{1,5},{5,9},{9,... | collective-permute-start | bytes 393224 | tf_op jit(solution)/shard_map/ppermute | solution.py:17
  243.3 9.1 %collective-permute-start.14 = (bf16[256,256]{0,1:T(8,128)(2,1)S(1)}, bf16[256,256]{0,1:T(8,128)(2,1)S(1)}, u32[]{:S(2)}, u32[]{:S(2)}) collective-permute-start(bf16[256,256]{0,1:T(8,128)(2,1)S(1)} %pad_maximum_fusion.3), channel_id=1, source_target_pairs={{4,0},{8,4},{12,8},{16,12},{20,16},{24,20},{28,24},{5,1},{9,5},{13... | collective-permute-start | bytes 393224 | tf_op jit(solution)/shard_map/ppermute | solution.py:17
  245.7 6.8 %collective-permute-start.15 = (bf16[256,256]{0,1:T(8,128)(2,1)S(1)}, bf16[256,256]{0,1:T(8,128)(2,1)S(1)}, u32[]{:S(2)}, u32[]{:S(2)}) collective-permute-start(bf16[256,256]{0,1:T(8,128)(2,1)S(1)} %pad_maximum_fusion.3), channel_id=1, source_target_pairs={{8,0},{12,4},{16,8},{20,12},{24,16},{28,20},{9,1},{13,5},{17,9},{2... | collective-permute-start | bytes 393224 | tf_op jit(solution)/shard_map/ppermute | solution.py:17
  (20 other events, 202.0 us)
Sparse Core Ops, SparseCore 0:
  9.6 35.4 all-gather.2
  260.7 17.1 all-gather.4
where the time goes:
time: 295 us; the launch traced here: 291 us
  blocking collectives  71.6 us (24%)
  local copies, waits for them, and re-layouts  56.3 us (19%)
  starting transfers between devices  53 us (18%)
  matrix products  50.4 us (17%)
  waiting for transfers between devices  29.4 us (10%)
  other arithmetic  15.3 us (5%)
  between operations  15 us (5%)
    ppermute x16, starting transfers between devices, from_behind(): lax.ppermute(value, axis, [(source, source + steps) for source in range(f...  48.1 us
    all_gather x1, blocking collectives, per_device(): lax.all_gather(mesh_in, 'mp', axis=1, tiled=True)  28.9 us
    all_gather x3, blocking collectives, mesh_update(): whole_new = lax.all_gather(part_new, 'mp', axis=1, tiled=True)  22 us
    unnamed x70, local copies, waits for them, and re-layouts  22 us
    all_gather x3, blocking collectives, mesh_update(): every_head = lax.all_gather(blended, 'mp', axis=1, tiled=True)  20.7 us
    dot_general x12, matrix products, project(): jnp.dot(inputs, weight, preferred_element_type=jnp.float32)  18.9 us
    all_gather x1, waiting for transfers between devices, per_device(): every_head = lax.all_gather(blended, 'mp', axis=1, tiled=True)  17.2 us
    ppermute x16, waiting for transfers between devices, from_behind(): lax.ppermute(value, axis, [(source, source + steps) for source in range(f...  11.5 us
  transfers between devices with their start and end apart: 19, of which 2 were waited for; matrix products, arithmetic and copies ran while one was open for 17% of the time, Pallas kernels for 0%

commit v1 on v0

v1 whole, which is shorter than its diff:
```python
import functools

import jax
import jax.numpy as jnp
from jax import lax
from jax.experimental import pallas as pl
from jax.experimental.pallas import tpu as pltpu
from jax.sharding import PartitionSpec as P

HEAD_DIM = 64
BLOCK = 128
REACH = 2
SLOTS = 2 * REACH + 1
EPS = 1e-05
NEG = -1e30
F32 = jnp.float32
BF16 = jnp.bfloat16
MESH = pl.DeviceIdType.MESH


def dot_nt(a, b):
    return lax.dot_general(a, b, (((1,), (1,)), ((), ())), preferred_element_type=F32)


def dot_nn(a, b):
    return jnp.dot(a, b, preferred_element_type=F32)


def kernel(
    sizes,
    enc_ref, proc_ref, dec_ref, count_ref,
    grid_ref, mesh_ref, wq_ref, wk_ref, wv_ref, wo_ref, gains_ref,
    gout_ref, mout_ref,
    gfull, mstate, wqkv, wofull, wolast, nbuf, nbuf2,
    qwin, member, kgrid, vtgrid, qdec, opart, stats, orecv, srecv,
    kvwins, oag, oagd,
    lsem, bsem_s, bsem_r, gsem_s, gsem_r, wsem_s, wsem_r, w3sem_s, w3sem_r,
    qsem_s, qsem_r, msem_s, msem_r, osem_s, osem_r, tsem_s, tsem_r,
    kvsem_s, kvsem_r, asem_s, asem_r, dsem_s, dsem_r,
):
    n_nodes, n_mp, chunks = sizes
    node = lax.axis_index("nodes")
    m = lax.axis_index("mp")
    rows_g, feat = grid_ref.shape
    rows_m = mesh_ref.shape[0]
    width = feat * n_mp
    hw = wq_ref.shape[2]
    heads = hw // HEAD_DIM
    gb = rows_g // BLOCK
    mb = rows_m // BLOCK
    chunk = rows_g // chunks
    cb = chunk // BLOCK
    layers = wq_ref.shape[0]
    peer = {1: m + 1 - 2 * (m % 2), 2: (m + 2) % 4, 3: 3 - m}

    def cols(who, size):
        return pl.ds(pl.multiple_of(who * size, size), size)

    def exists(off):
        return jnp.logical_and(node + off >= 0, node + off < n_nodes)

    pending = []

    def send_mp(src, dst, ssem, rsem, r):
        c = pltpu.make_async_remote_copy(
            src_ref=src, dst_ref=dst, send_sem=ssem, recv_sem=rsem,
            device_id={"mp": peer[r]}, device_id_type=MESH)
        c.start()
        pending.append(c)

    def recv_mp(ref, ssem, rsem, r):
        pltpu.make_async_remote_copy(
            src_ref=ref, dst_ref=ref, send_sem=ssem, recv_sem=rsem,
            device_id={"mp": peer[r]}, device_id_type=MESH).wait_recv()

    def node_copy(src, dst, ssem, rsem, off):
        return pltpu.make_async_remote_copy(
            src_ref=src, dst_ref=dst, send_sem=ssem, recv_sem=rsem,
            device_id={"nodes": node + off}, device_id_type=MESH)

    local = {}

    def load(name, src, dst, index):
        c = pltpu.make_async_copy(src, dst, lsem.at[index])
        c.start()
        local[name] = c

    load("mesh", mesh_ref, mstate.at[:, cols(m, feat)], 0)
    load("wq0", wq_ref.at[0], wqkv.at[0, :, 0:hw], 1)
    load("grid", grid_ref, gfull.at[:, cols(m, feat)], 2)
    load("wk", wk_ref, wqkv.at[:, :, hw:2 * hw], 3)
    load("wv", wv_ref, wqkv.at[:, :, 2 * hw:3 * hw], 4)
    load("wq1", wq_ref.at[1:layers], wqkv.at[1:layers, :, 0:hw], 5)
    load("wo", wo_ref.at[0:layers - 1], wofull.at[:, cols(m, hw), :], 6)
    load("wo3", wo_ref.at[layers - 1, :, cols(m, feat)], wolast.at[cols(m, hw), :], 7)

    for slot in range(SLOTS):
        off = slot - REACH
        if off == 0:
            continue

        @pl.when(jnp.logical_not(exists(off)))
        def _(slot=slot):
            orecv[slot] = jnp.zeros(orecv.shape[1:], BF16)
            srecv[slot] = jnp.full(srecv.shape[1:], NEG, F32)
            for l in range(layers - 1):
                kvwins[l][slot * mb:(slot + 1) * mb] = jnp.zeros((mb,) + kvwins[l].shape[1:], BF16)

    barrier = pltpu.get_barrier_semaphore()
    for r in (1, 2, 3):
        pl.semaphore_signal(barrier, inc=1, device_id={"mp": peer[r]}, device_id_type=MESH)
    for off in range(-REACH, REACH + 1):
        if off == 0:
            continue

        @pl.when(exists(off))
        def _(off=off):
            pl.semaphore_signal(barrier, inc=1, device_id={"nodes": node + off}, device_id_type=MESH)
    near = jnp.minimum(node, REACH) + jnp.minimum(n_nodes - 1 - node, REACH)
    pl.semaphore_wait(barrier, 3 + near)

    for r in (2, 1):
        send_mp(mesh_ref, mstate.at[:, cols(m, feat)], bsem_s.at[r - 1], bsem_r.at[r - 1], r)

    def grid_rows(c):
        return pl.ds(c * chunk, chunk)

    for c in range(chunks):
        for r in (2, 1):
            send_mp(grid_ref.at[grid_rows(c), :], gfull.at[grid_rows(c), cols(m, feat)],
                    gsem_s.at[c, r - 1], gsem_r.at[c, r - 1], r)

    def wo_send(l):
        for r in (2, 1):
            send_mp(wo_ref.at[l], wofull.at[l, cols(m, hw), :],
                    wsem_s.at[l, r - 1], wsem_r.at[l, r - 1], r)

    def wo_relay(l):
        part = wofull.at[l, cols(peer[2], hw), :]
        recv_mp(part, wsem_s.at[l, 1], wsem_r.at[l, 1], 2)
        send_mp(part, part, wsem_s.at[l, 2], wsem_r.at[l, 2], 1)

    def wo_finish(l):
        for r in (1, 3):
            recv_mp(wofull.at[l, cols(peer[r], hw), :], wsem_s.at[l, r - 1], wsem_r.at[l, r - 1], r)

    part = mstate.at[:, cols(peer[2], feat)]
    recv_mp(part, bsem_s.at[1], bsem_r.at[1], 2)
    send_mp(part, part, bsem_s.at[2], bsem_r.at[2], 1)
    state_relay = pending.pop()
    for r in (1, 3):
        recv_mp(mstate.at[:, cols(peer[r], feat)], bsem_s.at[r - 1], bsem_r.at[r - 1], r)
    local["mesh"].wait()

    def norm(src, start, count, targets, tile=64):
        def step(i, carry):
            at = pl.multiple_of(i * tile, tile)
            x = src[pl.ds(pl.multiple_of(start + at, tile), tile), :].astype(F32)
            x = x - jnp.mean(x, axis=-1, keepdims=True)
            spread = jnp.mean(x * x, axis=-1, keepdims=True)
            x = x * lax.rsqrt(spread + EPS)
            for dst, g in targets:
                dst[pl.ds(at, tile), :] = (x * gains_ref[g:g + 1, :]).astype(BF16)
            return carry
        lax.fori_loop(0, count // tile, step, 0)

    norm(mstate, 0, rows_m, [(nbuf, 0)])
    local["wq0"].wait()
    qwin[REACH] = (dot_nn(nbuf[0:rows_m, :], wqkv[0, :, 0:hw]).astype(BF16) * BF16(HEAD_DIM ** -0.5)).astype(BF16)

    own_block = lax.broadcasted_iota(jnp.int32, (gb, rows_m), 1) // BLOCK
    block_row = lax.broadcasted_iota(jnp.int32, (gb, rows_m), 0)

    def members(off):
        wanted = (node + off) * gb + block_row
        hit = jnp.zeros((gb, rows_m), jnp.bool_)
        for b in range(mb):
            for j in range(enc_ref.shape[1]):
                hit = hit | ((wanted == enc_ref[b, j]) & (own_block == b))
        return jnp.where(hit, 1.0, 0.0).astype(F32)

    member[REACH] = members(0)

    def q_copies(slot):
        off = slot - REACH
        a = node_copy(qwin.at[REACH], qwin.at[REACH - off], qsem_s.at[slot], qsem_r.at[REACH - off], off)
        b = node_copy(member.at[SLOTS + slot], member.at[REACH - off],
                      msem_s.at[slot], msem_r.at[REACH - off], off)
        return a, b

    remote_slots = [s for s in range(SLOTS) if s != REACH]
    for slot in remote_slots:
        @pl.when(exists(slot - REACH))
        def _(slot=slot):
            member[SLOTS + slot] = members(slot - REACH)
            for c in q_copies(slot):
                c.start()

    local["grid"].wait()
    local["wk"].wait()
    local["wv"].wait()
    local["wq1"].wait()

    def grid_chunk(c):
        norm(gfull, c * chunk, chunk, [(nbuf, 1), (nbuf2, 4)])
        kv = dot_nn(nbuf[0:chunk, :], wqkv[0, :, hw:3 * hw])
        kgrid[grid_rows(c), :] = kv[:, 0:hw].astype(BF16)
        vtgrid[:, c * chunk:(c + 1) * chunk] = kv[:, hw:].T.astype(BF16)
        qd = dot_nn(nbuf2[0:chunk, :], wqkv[layers - 1, :, 0:hw]).astype(BF16)
        qdec[grid_rows(c), :] = (qd * BF16(HEAD_DIM ** -0.5)).astype(BF16)

    for c in range(chunks + 1):
        if c < chunks:
            part = gfull.at[grid_rows(c), cols(peer[2], feat)]
            recv_mp(part, gsem_s.at[c, 1], gsem_r.at[c, 1], 2)
            send_mp(part, part, gsem_s.at[c, 2], gsem_r.at[c, 2], 1)
        if c == 0:
            wo_send(0)
        if c >= 1:
            for r in (1, 3):
                recv_mp(gfull.at[grid_rows(c - 1), cols(peer[r], feat)],
                        gsem_s.at[c - 1, r - 1], gsem_r.at[c - 1, r - 1], r)
            grid_chunk(c - 1)
    wo_relay(0)
    local["wo"].wait()

    lane_head = lax.broadcasted_iota(jnp.int32, (1, hw), 1) // HEAD_DIM
    row_in_block = lax.broadcasted_iota(jnp.int32, (BLOCK, 1), 0)

    def for_head(q, h):
        return jnp.where(lane_head == h, q, jnp.zeros_like(q))

    def o_copies(slot):
        back = slot - REACH
        a = node_copy(opart.at[slot], orecv.at[REACH - back], osem_s.at[slot], osem_r.at[REACH - back], back)
        b = node_copy(stats.at[slot], srecv.at[REACH - back], tsem_s.at[slot], tsem_r.at[REACH - back], back)
        return a, b

    def encode(i, carry):
        slot = i + i // 2 - 4 * (i // 4)
        off = slot - REACH
        remote = i < 2 * REACH

        @pl.when(jnp.logical_and(remote, exists(off)))
        def _():
            node_copy(qwin.at[slot], qwin.at[slot], qsem_s.at[slot], qsem_r.at[slot], off).wait_recv()
            node_copy(member.at[slot], member.at[slot], msem_s.at[slot], msem_r.at[slot], off).wait_recv()

        @pl.when(exists(off))
        def _():
            q = qwin[slot]
            listed = member[slot]
            for h in range(heads):
                qh = for_head(q, h)
                scores = []
                for c in range(gb):
                    ok = (row_in_block < count_ref[node * gb + c]) & (listed[c:c + 1, :] > 0.5)
                    s = dot_nt(kgrid[c * BLOCK:(c + 1) * BLOCK, :], qh)
                    scores.append(jnp.where(ok, s, NEG))
                top = functools.reduce(jnp.maximum, scores)
                top = jnp.max(top, axis=0, keepdims=True)
                probs = [jnp.exp(s - top) for s in scores]
                total = functools.reduce(jnp.add, probs)
                total = jnp.sum(total, axis=0, keepdims=True)
                p = jnp.concatenate([x.astype(BF16) for x in probs], axis=0)
                o = dot_nn(vtgrid[h * HEAD_DIM:(h + 1) * HEAD_DIM, :], p)
                opart[slot, h * HEAD_DIM:(h + 1) * HEAD_DIM, :] = o.astype(BF16)
                stats[slot, h:h + 1, :] = top
                stats[slot, heads + h:heads + h + 1, :] = total

        @pl.when(jnp.logical_and(remote, exists(off)))
        def _():
            for c in o_copies(slot):
                c.start()
        return carry

    lax.fori_loop(0, SLOTS, encode, 0)

    for slot in remote_slots:
        @pl.when(exists(slot - REACH))
        def _(slot=slot):
            off = slot - REACH
            node_copy(orecv.at[slot], orecv.at[slot], osem_s.at[slot], osem_r.at[slot], off).wait_recv()
            node_copy(srecv.at[slot], srecv.at[slot], tsem_s.at[slot], tsem_r.at[slot], off).wait_recv()

    merged = []
    for h in range(heads):
        tops = [stats[REACH, h:h + 1, :] if s == REACH else srecv[s, h:h + 1, :] for s in range(SLOTS)]
        sums = [stats[REACH, heads + h:heads + h + 1, :] if s == REACH else srecv[s, heads + h:heads + h + 1, :]
                for s in range(SLOTS)]
        top = functools.reduce(jnp.maximum, tops)
        total = jnp.zeros_like(top)
        blended = jnp.zeros((HEAD_DIM, rows_m), F32)
        for s in range(SLOTS):
            scale = jnp.exp(tops[s] - top)
            total = total + scale * sums[s]
            src = opart if s == REACH else orecv
            blended = blended + scale * src[s, h * HEAD_DIM:(h + 1) * HEAD_DIM, :].astype(F32)
        merged.append(blended / total)

    def mesh_update(l, merged_t):
        oag[l, :, cols(m, hw)] = merged_t.T.astype(BF16)
        for r in (2, 3, 1):
            src = oag.at[l, :, cols(m, hw)]
            send_mp(src, src, asem_s.at[l, r - 1], asem_r.at[l, r - 1], r)
        if l + 1 < layers - 1:
            wo_send(l + 1)
        else:
            for r in (2, 3, 1):
                send_mp(wo_ref.at[layers - 1, :, cols(peer[r], feat)], wolast.at[cols(m, hw), :],
                        w3sem_s.at[r - 1], w3sem_r.at[r - 1], r)
        wo_finish(l)
        for r in (1, 2, 3):
            recv_mp(oag.at[l, :, cols(peer[r], hw)], asem_s.at[l, r - 1], asem_r.at[l, r - 1], r)
        step = 256
        for j in range(0, width, step):
            update = dot_nn(oag[l], wofull[l, :, j:j + step])
            mstate[:, j:j + step] = (mstate[:, j:j + step].astype(F32) + update).astype(BF16)

    state_relay.wait_send()
    mesh_update(0, jnp.concatenate(merged, axis=0))

    def kv_copy(l, slot):
        off = slot - REACH
        return node_copy(kvwins[l].at[pl.ds(REACH * mb, mb)], kvwins[l].at[pl.ds((REACH - off) * mb, mb)],
                         kvsem_s.at[l, slot], kvsem_r.at[l, REACH - off], off)

    def spread_kv(l, weight_layer):
        kv = dot_nn(nbuf[0:rows_m, :], wqkv[weight_layer, :, hw:3 * hw])
        vt = kv[:, hw:].T
        for b in range(mb):
            kvwins[l][REACH * mb + b, 0] = kv[b * BLOCK:(b + 1) * BLOCK, 0:hw].astype(BF16)
            kvwins[l][REACH * mb + b, 1] = vt[:, b * BLOCK:(b + 1) * BLOCK].astype(BF16)
        for slot in remote_slots:
            @pl.when(exists(slot - REACH))
            def _(slot=slot):
                kv_copy(l, slot).start()

    def collect_kv(l):
        for slot in remote_slots:
            @pl.when(exists(slot - REACH))
            def _(slot=slot):
                part = kvwins[l].at[pl.ds(slot * mb, mb)]
                node_copy(part, part, kvsem_s.at[l, slot], kvsem_r.at[l, slot], slot - REACH).wait_recv()

    def attend(l, q, places):
        keys = jnp.concatenate([kvwins[l][at, 0] for at in places], axis=0)
        values_t = jnp.concatenate([kvwins[l][at, 1] for at in places], axis=1)
        out = []
        for h in range(heads):
            s = dot_nt(keys, for_head(q, h))
            p = jnp.exp(s - jnp.max(s, axis=0, keepdims=True))
            total = jnp.sum(p, axis=0, keepdims=True)
            o = dot_nn(values_t[h * HEAD_DIM:(h + 1) * HEAD_DIM, :], p.astype(BF16))
            out.append(o / total)
        return jnp.concatenate(out, axis=0)

    def place(block):
        return jnp.clip(block - (node - REACH) * mb, 0, SLOTS * mb - 1)

    for l in range(1, layers - 1):
        norm(mstate, 0, rows_m, [(nbuf, l + 1)])
        spread_kv(l - 1, l)
        q = dot_nn(nbuf[0:rows_m, :], wqkv[l, :, 0:hw]).astype(BF16)
        q = (q * BF16(HEAD_DIM ** -0.5)).astype(BF16)
        wo_relay(l)
        collect_kv(l - 1)
        blended = []
        for b in range(mb):
            places = [place(proc_ref[b, j]) for j in range(proc_ref.shape[1])]
            blended.append(attend(l - 1, q[b * BLOCK:(b + 1) * BLOCK, :], places))
        mesh_update(l, jnp.concatenate(blended, axis=1))

    last = layers - 2
    norm(mstate, 0, rows_m, [(nbuf, layers + 1)])
    spread_kv(last, layers - 1)
    mout_ref[...] = mstate[:, cols(m, feat)]
    local["wo3"].wait()
    for r in (1, 2, 3):
        recv_mp(wolast.at[cols(peer[r], hw), :], w3sem_s.at[r - 1], w3sem_r.at[r - 1], r)
    collect_kv(last)
    for c in range(chunks):
        for b in range(c * cb, (c + 1) * cb):
            places = [place(dec_ref[b, j]) for j in range(dec_ref.shape[1])]
            rows = slice(b * BLOCK, (b + 1) * BLOCK)
            oagd[rows, cols(m, hw)] = attend(last, qdec[rows, :], places).T.astype(BF16)
        src = oagd.at[grid_rows(c), cols(m, hw)]
        for r in (2, 1):
            send_mp(src, src, dsem_s.at[c, r - 1], dsem_r.at[c, r - 1], r)
        if c >= 1:
            part = oagd.at[grid_rows(c - 1), cols(peer[2], hw)]
            recv_mp(part, dsem_s.at[c - 1, 1], dsem_r.at[c - 1, 1], 2)
            send_mp(part, part, dsem_s.at[c - 1, 2], dsem_r.at[c - 1, 2], 1)
    for c in range(chunks):
        if c == chunks - 1:
            part = oagd.at[grid_rows(c), cols(peer[2], hw)]
            recv_mp(part, dsem_s.at[c, 1], dsem_r.at[c, 1], 2)
            send_mp(part, part, dsem_s.at[c, 2], dsem_r.at[c, 2], 1)
        for r in (1, 3):
            recv_mp(oagd.at[grid_rows(c), cols(peer[r], hw)], dsem_s.at[c, r - 1], dsem_r.at[c, r - 1], r)
        update = dot_nn(oagd[grid_rows(c), :], wolast[...])
        whole = gfull[grid_rows(c), cols(m, feat)].astype(F32) + update
        for b in range(cb):
            ok = row_in_block < count_ref[node * gb + c * cb + b]
            piece = jnp.where(ok, whole[b * BLOCK:(b + 1) * BLOCK, :], 0.0)
            gout_ref[pl.ds((c * cb + b) * BLOCK, BLOCK), :] = piece.astype(BF16)

    for c in pending:
        c.wait_send()
    for slot in remote_slots:
        @pl.when(exists(slot - REACH))
        def _(slot=slot):
            for c in q_copies(slot) + o_copies(slot):
                c.wait_send()
            for l in range(layers - 1):
                kv_copy(l, slot).wait_send()


def per_device(n_nodes, n_mp, grid_in, mesh_in, w_query, w_key, w_value, w_out, norm_gains,
               enc_list, proc_list, dec_list, grid_count):
    rows_g, feat = grid_in.shape
    rows_m = mesh_in.shape[0]
    width = feat * n_mp
    layers, _, hw = w_query.shape
    heads = hw // HEAD_DIM
    gb, mb = rows_g // BLOCK, rows_m // BLOCK
    chunks = gb // 2 if gb % 2 == 0 else gb
    chunk = rows_g // chunks
    norm_rows = max(chunk, rows_m)
    dma = lambda *shape: pltpu.SemaphoreType.DMA(shape)
    vm = pltpu.VMEM
    scratch = [
        vm((rows_g, width), BF16),
        vm((rows_m, width), BF16),
        vm((layers, width, 3 * hw), BF16),
        vm((layers - 1, hw * n_mp, width), BF16),
        vm((hw * n_mp, feat), BF16),
        vm((norm_rows, width), BF16),
        vm((norm_rows, width), BF16),
        vm((SLOTS, rows_m, hw), BF16),
        vm((2 * SLOTS, gb, rows_m), F32),
        vm((rows_g, hw), BF16),
        vm((hw, rows_g), BF16),
        vm((rows_g, hw), BF16),
        vm((SLOTS, hw, rows_m), BF16),
        vm((SLOTS, max(8, 2 * heads), rows_m), F32),
        vm((SLOTS, hw, rows_m), BF16),
        vm((SLOTS, max(8, 2 * heads), rows_m), F32),
        [vm((SLOTS * mb, 2, BLOCK, hw), BF16) for _ in range(layers - 1)],
        vm((layers - 1, rows_m, hw * n_mp), BF16),
        vm((rows_g, hw * n_mp), BF16),
        dma(8), dma(3), dma(3), dma(chunks, 3), dma(chunks, 3),
        dma(layers - 1, 3), dma(layers - 1, 3), dma(3), dma(3),
        dma(SLOTS), dma(SLOTS), dma(SLOTS), dma(SLOTS), dma(SLOTS), dma(SLOTS), dma(SLOTS), dma(SLOTS),
        dma(layers - 1, SLOTS), dma(layers - 1, SLOTS), dma(layers - 1, 3), dma(layers - 1, 3),
        dma(chunks, 3), dma(chunks, 3),
    ]
    smem = pl.BlockSpec(memory_space=pltpu.SMEM)
    anyspace = pl.BlockSpec(memory_space=pl.ANY)
    vmem = pl.BlockSpec(memory_space=pltpu.VMEM)
    return pl.pallas_call(
        functools.partial(kernel, (n_nodes, n_mp, chunks)),
        out_shape=(
            jax.ShapeDtypeStruct(grid_in.shape, BF16),
            jax.ShapeDtypeStruct(mesh_in.shape, BF16),
        ),
        in_specs=[smem] * 4 + [anyspace] * 6 + [vmem],
        out_specs=(vmem, vmem),
        scratch_shapes=scratch,
        compiler_params=pltpu.CompilerParams(
            collective_id=0, has_side_effects=True, vmem_limit_bytes=60 * 1024 * 1024
        ),
    )(enc_list, proc_list, dec_list, grid_count, grid_in, mesh_in, w_query, w_key, w_value, w_out, norm_gains)


def solution(mesh):
    placed = (
        P("nodes", "mp"),
        P("nodes", "mp"),
        P(None, None, "mp"),
        P(None, None, "mp"),
        P(None, None, "mp"),
        P(None, "mp", None),
        P(),
        P("nodes", None),
        P("nodes", None),
        P("nodes", None),
        P(),
    )
    return jax.shard_map(
        functools.partial(per_device, mesh.shape["nodes"], mesh.shape["mp"]),
        mesh=mesh,
        in_specs=placed,
        out_specs=(P("nodes", "mp"), P("nodes", "mp")),
        check_vma=False,
    )
```

time: 295 us -> 97 us (0.33); the launches traced: 291 us -> 96.8 us
  Pallas kernels: 0 us -> 92.3 us
  blocking collectives: 71.6 us -> 0 us
  starting transfers between devices: 53 us -> 0 us
  local copies, waits for them, and re-layouts: 56.3 us -> 3.91 us
  matrix products: 50.4 us -> 0 us
  waiting for transfers between devices: 29.4 us -> 0 us
  other arithmetic: 15.3 us -> 0 us
  between operations: 15 us -> 0.65 us
    pallas_call x0 -> x1, Pallas kernels: none -> 92.3 us  [per_device(): pl.pallas_call(functools.partial(kernel, (n_nodes, n_mp, chunks)), out_sh...]
    all_gather x7 -> x0, blocking collectives: 71.6 us -> none  [the longest x1 28.9 us: per_device(): lax.all_gather(mesh_in, 'mp', axis=1, tiled=True)]
    ppermute x16 -> x0, starting transfers between devices: 48.1 us -> none  [from_behind(): lax.ppermute(value, axis, [(source, source + steps) for source in range(f...]
    dot_general x35 -> x0, matrix products: 44.1 us -> none  [the longest x12 18.9 us: project(): jnp.dot(inputs, weight, preferred_element_type=jnp.float32)]
    unnamed x70 -> x5, local copies, waits for them, and re-layouts: 22 us -> 3.91 us
    all_gather x2 -> x0, waiting for transfers between devices: 17.2 us -> none  [the longest x1 17.2 us: per_device(): every_head = lax.all_gather(blended, 'mp', axis=1, tiled=True)]
    ppermute x16 -> x0, waiting for transfers between devices: 11.5 us -> none  [from_behind(): lax.ppermute(value, axis, [(source, source + steps) for source in range(f...]
    gather x6 -> x0, local copies, waits for them, and re-layouts: 9.73 us -> none  [pick(): chosen = jnp.take(blocks, local_ids, axis=0)]
  transfers between devices with their start and end apart: 19 -> 0, of which waited for: 2 -> 0; matrix products, arithmetic and copies ran while one was open for 17% -> 0% of each run, Pallas kernels for 0% -> 0%
where the time goes in v1:
time: 97 us; the launch traced here: 96.8 us
  Pallas kernels  92.3 us (95%)
  local copies, waits for them, and re-layouts  3.91 us (4%)
    pallas_call x1, Pallas kernels, per_device(): pl.pallas_call(functools.partial(kernel, (n_nodes, n_mp, chunks)), out_sh...  92.3 us
    unnamed x5, local copies, waits for them, and re-layouts  3.91 us

profile of v1, /device:TPU:11, one launch (start us, length us, event | category | flops | bytes accessed | tf_op | source)
XLA Modules:
  0.0 96.8 jit_solution(2495047143255407893)
XLA Ops:
  0.6 1.3 %copy.13.dec_ref = s32[8,2]{1,0:T(8,128)} copy(s32[8,2]{0,1:T(2,128)} %param.20) | data formatting | bytes 128 | tf_op args[9]
  2.0 92.3 %shard_map.122 = (bf16[1024,256]{1,0:T(8,128)(2,1)}, bf16[256,256]{1,0:T(8,128)(2,1)}) custom-call(s32[2,4]{1,0:T(2,128)} %enc_ref.1, s32[2,3]{1,0:T(2,128)} %proc_ref.1, s32[8,2]{1,0:T(8,128)} %copy.13.dec_ref, s32[64]{0:T(128)} %count_ref.1, bf16[1024,256]{1,0:T(8,128)(2,1)} %grid_ref.1, bf16[256,256]{1,0:T(8,128)(2,1)} %mesh_ref.1, ...), custom_call_target="tpu_custom_call" | custom-call | tf_op jit(solution)/shard_map/pallas_call | solution.py:461
  94.2 0.0 copy-start
  94.3 1.9 %copy.16 = bf16[1024,256]{1,0:T(8,128)(2,1)} copy(bf16[1024,256]{1,0:T(8,128)(2,1)} %get-tuple-element.4) | data formatting | bytes 1048576
  96.2 0.0 copy-done
  96.2 0.7 copy.17
Async XLA Ops:
  94.2 1.9 %copy-start = (bf16[256,256]{1,0:T(8,128)(2,1)S(1)}, bf16[256,256]{1,0:T(8,128)(2,1)}, u32[]{:S(2)}) copy-start(bf16[256,256]{1,0:T(8,128)(2,1)} %get-tuple-element.5) | copy-start | bytes 393220

commit v2 on v1

--- a/solution.py
+++ b/solution.py
@@ -283,65 +283,63 @@
             node_copy(orecv.at[slot], orecv.at[slot], osem_s.at[slot], osem_r.at[slot], off).wait_recv()
             node_copy(srecv.at[slot], srecv.at[slot], tsem_s.at[slot], tsem_r.at[slot], off).wait_recv()
 
-    merged = []
-    for h in range(heads):
-        tops = [stats[REACH, h:h + 1, :] if s == REACH else srecv[s, h:h + 1, :] for s in range(SLOTS)]
-        sums = [stats[REACH, heads + h:heads + h + 1, :] if s == REACH else srecv[s, heads + h:heads + h + 1, :]
-                for s in range(SLOTS)]
-        top = functools.reduce(jnp.maximum, tops)
-        total = jnp.zeros_like(top)
-        blended = jnp.zeros((HEAD_DIM, rows_m), F32)
-        for s in range(SLOTS):
-            scale = jnp.exp(tops[s] - top)
-            total = total + scale * sums[s]
-            src = opart if s == REACH else orecv
-            blended = blended + scale * src[s, h * HEAD_DIM:(h + 1) * HEAD_DIM, :].astype(F32)
-        merged.append(blended / total)
-
-    def mesh_update(l, merged_t):
-        oag[l, :, cols(m, hw)] = merged_t.T.astype(BF16)
+    def merge(b):
+        lanes = slice(b * BLOCK, (b + 1) * BLOCK)
+        merged = []
+        for h in range(heads):
+            rows = slice(h * HEAD_DIM, (h + 1) * HEAD_DIM)
+            tops, sums, parts = [], [], []
+            for s in range(SLOTS):
+                st, part = (stats, opart) if s == REACH else (srecv, orecv)
+                tops.append(st[s, h:h + 1, lanes])
+                sums.append(st[s, heads + h:heads + h + 1, lanes])
+                parts.append(part[s, rows, lanes].astype(F32))
+            top = functools.reduce(jnp.maximum, tops)
+            scales = [jnp.exp(t - top) for t in tops]
+            total = functools.reduce(jnp.add, [a * x for a, x in zip(scales, sums)])
+            blended = functools.reduce(jnp.add, [a * x for a, x in zip(scales, parts)])
+            merged.append(blended / total)
+        return jnp.concatenate(merged, axis=0)
+
+    def block_rows(b):
+        return pl.ds(b * BLOCK, BLOCK)
+
+    def share(l, b, blended_t):
+        src = oag.at[l, block_rows(b), cols(m, hw)]
+        oag[l, block_rows(b), cols(m, hw)] = blended_t.T.astype(BF16)
         for r in (2, 3, 1):
-            src = oag.at[l, :, cols(m, hw)]
-            send_mp(src, src, asem_s.at[l, r - 1], asem_r.at[l, r - 1], r)
-        if l + 1 < layers - 1:
-            wo_send(l + 1)
-        else:
-            for r in (2, 3, 1):
-                send_mp(wo_ref.at[layers - 1, :, cols(peer[r], feat)], wolast.at[cols(m, hw), :],
-                        w3sem_s.at[r - 1], w3sem_r.at[r - 1], r)
-        wo_finish(l)
+            send_mp(src, src, asem_s.at[l, b, r - 1], asem_r.at[l, b, r - 1], r)
+
+    def kv_copy(l, slot, b):
+        off = slot - REACH
+        return node_copy(kvwins[l].at[REACH * mb + b], kvwins[l].at[(REACH - off) * mb + b],
+                         kvsem_s.at[l, slot, b], kvsem_r.at[l, REACH - off, b], off)
+
+    def update(l, b):
         for r in (1, 2, 3):
-            recv_mp(oag.at[l, :, cols(peer[r], hw)], asem_s.at[l, r - 1], asem_r.at[l, r - 1], r)
+            recv_mp(oag.at[l, block_rows(b), cols(peer[r], hw)],
+                    asem_s.at[l, b, r - 1], asem_r.at[l, b, r - 1], r)
         step = 256
         for j in range(0, width, step):
-            update = dot_nn(oag[l], wofull[l, :, j:j + step])
-            mstate[:, j:j + step] = (mstate[:, j:j + step].astype(F32) + update).astype(BF16)
-
-    state_relay.wait_send()
-    mesh_update(0, jnp.concatenate(merged, axis=0))
-
-    def kv_copy(l, slot):
-        off = slot - REACH
-        return node_copy(kvwins[l].at[pl.ds(REACH * mb, mb)], kvwins[l].at[pl.ds((REACH - off) * mb, mb)],
-                         kvsem_s.at[l, slot], kvsem_r.at[l, REACH - off], off)
-
-    def spread_kv(l, weight_layer):
-        kv = dot_nn(nbuf[0:rows_m, :], wqkv[weight_layer, :, hw:3 * hw])
-        vt = kv[:, hw:].T
-        for b in range(mb):
-            kvwins[l][REACH * mb + b, 0] = kv[b * BLOCK:(b + 1) * BLOCK, 0:hw].astype(BF16)
-            kvwins[l][REACH * mb + b, 1] = vt[:, b * BLOCK:(b + 1) * BLOCK].astype(BF16)
+            change = dot_nn(oag[l, block_rows(b), :], wofull[l, :, j:j + step])
+            mstate[block_rows(b), j:j + step] = (mstate[block_rows(b), j:j + step].astype(F32) + change).astype(BF16)
+        norm(mstate, b * BLOCK, BLOCK, [(nbuf.at[block_rows(b), :], l + 2 if l + 2 < layers else layers + 1)])
+        kv = dot_nn(nbuf[block_rows(b), :], wqkv[l + 1, :, hw:3 * hw])
+        kvwins[l][REACH * mb + b, 0] = kv[:, 0:hw].astype(BF16)
+        kvwins[l][REACH * mb + b, 1] = kv[:, hw:].T.astype(BF16)
         for slot in remote_slots:
             @pl.when(exists(slot - REACH))
             def _(slot=slot):
-                kv_copy(l, slot).start()
+                kv_copy(l, slot, b).start()
 
     def collect_kv(l):
         for slot in remote_slots:
             @pl.when(exists(slot - REACH))
             def _(slot=slot):
-                part = kvwins[l].at[pl.ds(slot * mb, mb)]
-                node_copy(part, part, kvsem_s.at[l, slot], kvsem_r.at[l, slot], slot - REACH).wait_recv()
+                for b in range(mb):
+                    part = kvwins[l].at[slot * mb + b]
+                    node_copy(part, part, kvsem_s.at[l, slot, b], kvsem_r.at[l, slot, b],
+                              slot - REACH).wait_recv()
 
     def attend(l, q, places):
         keys = jnp.concatenate([kvwins[l][at, 0] for at in places], axis=0)
@@ -358,22 +356,31 @@
     def place(block):
         return jnp.clip(block - (node - REACH) * mb, 0, SLOTS * mb - 1)
 
-    for l in range(1, layers - 1):
-        norm(mstate, 0, rows_m, [(nbuf, l + 1)])
-        spread_kv(l - 1, l)
-        q = dot_nn(nbuf[0:rows_m, :], wqkv[l, :, 0:hw]).astype(BF16)
-        q = (q * BF16(HEAD_DIM ** -0.5)).astype(BF16)
-        wo_relay(l)
-        collect_kv(l - 1)
-        blended = []
+    state_relay.wait_send()
+    for l in range(layers - 1):
+        if l > 0:
+            q = dot_nn(nbuf[0:rows_m, :], wqkv[l, :, 0:hw]).astype(BF16)
+            q = (q * BF16(HEAD_DIM ** -0.5)).astype(BF16)
+            wo_relay(l)
+            collect_kv(l - 1)
         for b in range(mb):
-            places = [place(proc_ref[b, j]) for j in range(proc_ref.shape[1])]
-            blended.append(attend(l - 1, q[b * BLOCK:(b + 1) * BLOCK, :], places))
-        mesh_update(l, jnp.concatenate(blended, axis=1))
+            if l == 0:
+                blended_t = merge(b)
+            else:
+                places = [place(proc_ref[b, j]) for j in range(proc_ref.shape[1])]
+                blended_t = attend(l - 1, q[b * BLOCK:(b + 1) * BLOCK, :], places)
+            share(l, b, blended_t)
+        if l + 1 < layers - 1:
+            wo_send(l + 1)
+        else:
+            for r in (2, 3, 1):
+                send_mp(wo_ref.at[layers - 1, :, cols(peer[r], feat)], wolast.at[cols(m, hw), :],
+                        w3sem_s.at[r - 1], w3sem_r.at[r - 1], r)
+        wo_finish(l)
+        for b in range(mb):
+            update(l, b)
 
     last = layers - 2
-    norm(mstate, 0, rows_m, [(nbuf, layers + 1)])
-    spread_kv(last, layers - 1)
     mout_ref[...] = mstate[:, cols(m, feat)]
     local["wo3"].wait()
     for r in (1, 2, 3):
@@ -398,8 +405,8 @@
             send_mp(part, part, dsem_s.at[c, 2], dsem_r.at[c, 2], 1)
         for r in (1, 3):
             recv_mp(oagd.at[grid_rows(c), cols(peer[r], hw)], dsem_s.at[c, r - 1], dsem_r.at[c, r - 1], r)
-        update = dot_nn(oagd[grid_rows(c), :], wolast[...])
-        whole = gfull[grid_rows(c), cols(m, feat)].astype(F32) + update
+        change = dot_nn(oagd[grid_rows(c), :], wolast[...])
+        whole = gfull[grid_rows(c), cols(m, feat)].astype(F32) + change
         for b in range(cb):
             ok = row_in_block < count_ref[node * gb + c * cb + b]
             piece = jnp.where(ok, whole[b * BLOCK:(b + 1) * BLOCK, :], 0.0)
@@ -413,7 +420,8 @@
             for c in q_copies(slot) + o_copies(slot):
                 c.wait_send()
             for l in range(layers - 1):
-                kv_copy(l, slot).wait_send()
+                for b in range(mb):
+                    kv_copy(l, slot, b).wait_send()
 
 
 def per_device(n_nodes, n_mp, grid_in, mesh_in, w_query, w_key, w_value, w_out, norm_gains,
@@ -452,7 +460,7 @@
         dma(8), dma(3), dma(3), dma(chunks, 3), dma(chunks, 3),
         dma(layers - 1, 3), dma(layers - 1, 3), dma(3), dma(3),
         dma(SLOTS), dma(SLOTS), dma(SLOTS), dma(SLOTS), dma(SLOTS), dma(SLOTS), dma(SLOTS), dma(SLOTS),
-        dma(layers - 1, SLOTS), dma(layers - 1, SLOTS), dma(layers - 1, 3), dma(layers - 1, 3),
+        dma(layers - 1, SLOTS, mb), dma(layers - 1, SLOTS, mb), dma(layers - 1, mb, 3), dma(layers - 1, mb, 3),
         dma(chunks, 3), dma(chunks, 3),
     ]
     smem = pl.BlockSpec(memory_space=pltpu.SMEM)

time: 97 us -> 92.2 us (0.951)
  Pallas kernels: 92.3 us -> 87.4 us
    pallas_call x1, Pallas kernels: 92.3 us -> 87.4 us  [per_device(): pl.pallas_call(functools.partial(kernel, (n_nodes, n_mp, chunks)), out_sh...]
where the time goes in v2:
time: 92.2 us; the launch traced here: 92 us
  Pallas kernels  87.4 us (95%)
  local copies, waits for them, and re-layouts  3.91 us (4%)
    pallas_call x1, Pallas kernels, per_device(): pl.pallas_call(functools.partial(kernel, (n_nodes, n_mp, chunks)), out_sh...  87.4 us
    unnamed x5, local copies, waits for them, and re-layouts  3.91 us

profile of v2, /device:TPU:11, one launch (start us, length us, event | category | flops | bytes accessed | tf_op | source)
XLA Modules:
  0.0 92.0 jit_solution(9930041637313929073)
XLA Ops:
  0.6 1.3 %copy.13.dec_ref = s32[8,2]{1,0:T(8,128)} copy(s32[8,2]{0,1:T(2,128)} %param.20) | data formatting | bytes 128 | tf_op args[9]
  2.0 87.4 %shard_map.122 = (bf16[1024,256]{1,0:T(8,128)(2,1)}, bf16[256,256]{1,0:T(8,128)(2,1)}) custom-call(s32[2,4]{1,0:T(2,128)} %enc_ref.1, s32[2,3]{1,0:T(2,128)} %proc_ref.1, s32[8,2]{1,0:T(8,128)} %copy.13.dec_ref, s32[64]{0:T(128)} %count_ref.1, bf16[1024,256]{1,0:T(8,128)(2,1)} %grid_ref.1, bf16[256,256]{1,0:T(8,128)(2,1)} %mesh_ref.1, ...), custom_call_target="tpu_custom_call" | custom-call | tf_op jit(solution)/shard_map/pallas_call | solution.py:469
  89.4 0.0 copy-start
  89.4 1.9 %copy.16 = bf16[1024,256]{1,0:T(8,128)(2,1)} copy(bf16[1024,256]{1,0:T(8,128)(2,1)} %get-tuple-element.4) | data formatting | bytes 1048576
  91.3 0.0 copy-done
  91.3 0.7 copy.17
Async XLA Ops:
  89.4 1.9 %copy-start = (bf16[256,256]{1,0:T(8,128)(2,1)S(1)}, bf16[256,256]{1,0:T(8,128)(2,1)}, u32[]{:S(2)}) copy-start(bf16[256,256]{1,0:T(8,128)(2,1)} %get-tuple-element.5) | copy-start | bytes 393220

commit v3 on v2

--- a/solution.py
+++ b/solution.py
@@ -32,7 +32,7 @@
     grid_ref, mesh_ref, wq_ref, wk_ref, wv_ref, wo_ref, gains_ref,
     gout_ref, mout_ref,
     gfull, mstate, wqkv, wofull, wolast, nbuf, nbuf2,
-    qwin, member, kgrid, vtgrid, qdec, opart, stats, orecv, srecv,
+    qwin, member, kgrid, vtgrid, qdec, opart, oearly, stats, orecv, srecv,
     kvwins, oag, oagd,
     lsem, bsem_s, bsem_r, gsem_s, gsem_r, wsem_s, wsem_r, w3sem_s, w3sem_r,
     qsem_s, qsem_r, msem_s, msem_r, osem_s, osem_r, tsem_s, tsem_r,
@@ -209,6 +209,69 @@
         qd = dot_nn(nbuf2[0:chunk, :], wqkv[layers - 1, :, 0:hw]).astype(BF16)
         qdec[grid_rows(c), :] = (qd * BF16(HEAD_DIM ** -0.5)).astype(BF16)
 
+    lane_head = lax.broadcasted_iota(jnp.int32, (1, hw), 1) // HEAD_DIM
+    row_in_block = lax.broadcasted_iota(jnp.int32, (BLOCK, 1), 0)
+
+    def for_head(q, h):
+        return jnp.where(lane_head == h, q, jnp.zeros_like(q))
+
+    def o_copies(slot):
+        back = slot - REACH
+        a = node_copy(opart.at[slot], orecv.at[REACH - back], osem_s.at[slot], osem_r.at[REACH - back], back)
+        b = node_copy(stats.at[slot], srecv.at[REACH - back], tsem_s.at[slot], tsem_r.at[REACH - back], back)
+        return a, b
+
+    half = gb // 2
+
+    def encode(late, i, carry):
+        slot = i + i // 2 - 4 * (i // 4)
+        off = slot - REACH
+        remote = i < 2 * REACH
+
+        @pl.when(jnp.logical_and(remote, exists(off)) if not late else False)
+        def _():
+            node_copy(qwin.at[slot], qwin.at[slot], qsem_s.at[slot], qsem_r.at[slot], off).wait_recv()
+            node_copy(member.at[slot], member.at[slot], msem_s.at[slot], msem_r.at[slot], off).wait_recv()
+
+        @pl.when(exists(off))
+        def _():
+            q = qwin[slot]
+            listed = member[slot]
+            for h in range(heads):
+                qh = for_head(q, h)
+                scores = []
+                blocks = range(half, gb) if late else range(half)
+                for c in blocks:
+                    ok = (row_in_block < count_ref[node * gb + c]) & (listed[c:c + 1, :] > 0.5)
+                    s = dot_nt(kgrid[c * BLOCK:(c + 1) * BLOCK, :], qh)
+                    scores.append(jnp.where(ok, s, NEG))
+                top = functools.reduce(jnp.maximum, scores)
+                top = jnp.max(top, axis=0, keepdims=True)
+                if late:
+                    before = stats[slot, h:h + 1, :]
+                    top = jnp.maximum(top, before)
+                probs = [jnp.exp(s - top) for s in scores]
+                total = functools.reduce(jnp.add, probs)
+                total = jnp.sum(total, axis=0, keepdims=True)
+                p = jnp.concatenate([x.astype(BF16) for x in probs], axis=0)
+                keys = slice(blocks[0] * BLOCK, (blocks[-1] + 1) * BLOCK)
+                o = dot_nn(vtgrid[h * HEAD_DIM:(h + 1) * HEAD_DIM, keys], p)
+                if late:
+                    scale = jnp.exp(before - top)
+                    total = total + scale * stats[slot, heads + h:heads + h + 1, :]
+                    o = o + scale * oearly[slot, h * HEAD_DIM:(h + 1) * HEAD_DIM, :]
+                    opart[slot, h * HEAD_DIM:(h + 1) * HEAD_DIM, :] = o.astype(BF16)
+                else:
+                    oearly[slot, h * HEAD_DIM:(h + 1) * HEAD_DIM, :] = o
+                stats[slot, h:h + 1, :] = top
+                stats[slot, heads + h:heads + h + 1, :] = total
+
+        @pl.when(jnp.logical_and(remote, exists(off)) if late else False)
+        def _():
+            for c in o_copies(slot):
+                c.start()
+        return carry
+
     for c in range(chunks + 1):
         if c < chunks:
             part = gfull.at[grid_rows(c), cols(peer[2], feat)]
@@ -221,60 +284,11 @@
                 recv_mp(gfull.at[grid_rows(c - 1), cols(peer[r], feat)],
                         gsem_s.at[c - 1, r - 1], gsem_r.at[c - 1, r - 1], r)
             grid_chunk(c - 1)
+            if c == half // cb:
+                lax.fori_loop(0, SLOTS, functools.partial(encode, False), 0)
+    lax.fori_loop(0, SLOTS, functools.partial(encode, True), 0)
     wo_relay(0)
     local["wo"].wait()
-
-    lane_head = lax.broadcasted_iota(jnp.int32, (1, hw), 1) // HEAD_DIM
-    row_in_block = lax.broadcasted_iota(jnp.int32, (BLOCK, 1), 0)
-
-    def for_head(q, h):
-        return jnp.where(lane_head == h, q, jnp.zeros_like(q))
-
-    def o_copies(slot):
-        back = slot - REACH
-        a = node_copy(opart.at[slot], orecv.at[REACH - back], osem_s.at[slot], osem_r.at[REACH - back], back)
-        b = node_copy(stats.at[slot], srecv.at[REACH - back], tsem_s.at[slot], tsem_r.at[REACH - back], back)
-        return a, b
-
-    def encode(i, carry):
-        slot = i + i // 2 - 4 * (i // 4)
-        off = slot - REACH
-        remote = i < 2 * REACH
-
-        @pl.when(jnp.logical_and(remote, exists(off)))
-        def _():
-            node_copy(qwin.at[slot], qwin.at[slot], qsem_s.at[slot], qsem_r.at[slot], off).wait_recv()
-            node_copy(member.at[slot], member.at[slot], msem_s.at[slot], msem_r.at[slot], off).wait_recv()
-
-        @pl.when(exists(off))
-        def _():
-            q = qwin[slot]
-            listed = member[slot]
-            for h in range(heads):
-                qh = for_head(q, h)
-                scores = []
-                for c in range(gb):
-                    ok = (row_in_block < count_ref[node * gb + c]) & (listed[c:c + 1, :] > 0.5)
-                    s = dot_nt(kgrid[c * BLOCK:(c + 1) * BLOCK, :], qh)
-                    scores.append(jnp.where(ok, s, NEG))
-                top = functools.reduce(jnp.maximum, scores)
-                top = jnp.max(top, axis=0, keepdims=True)
-                probs = [jnp.exp(s - top) for s in scores]
-                total = functools.reduce(jnp.add, probs)
-                total = jnp.sum(total, axis=0, keepdims=True)
-                p = jnp.concatenate([x.astype(BF16) for x in probs], axis=0)
-                o = dot_nn(vtgrid[h * HEAD_DIM:(h + 1) * HEAD_DIM, :], p)
-                opart[slot, h * HEAD_DIM:(h + 1) * HEAD_DIM, :] = o.astype(BF16)
-                stats[slot, h:h + 1, :] = top
-                stats[slot, heads + h:heads + h + 1, :] = total
-
-        @pl.when(jnp.logical_and(remote, exists(off)))
-        def _():
-            for c in o_copies(slot):
-                c.start()
-        return carry
-
-    lax.fori_loop(0, SLOTS, encode, 0)
 
     for slot in remote_slots:
         @pl.when(exists(slot - REACH))
@@ -451,6 +465,7 @@
         vm((hw, rows_g), BF16),
         vm((rows_g, hw), BF16),
         vm((SLOTS, hw, rows_m), BF16),
+        vm((SLOTS, hw, rows_m), F32),
         vm((SLOTS, max(8, 2 * heads), rows_m), F32),
         vm((SLOTS, hw, rows_m), BF16),
         vm((SLOTS, max(8, 2 * heads), rows_m), F32),

time: 92.2 us -> 91.6 us (level)
  no operation moved by 1% of the time
where the time goes in v3:
time: 91.6 us; the launch traced here: 91.4 us
  Pallas kernels  86.9 us (95%)
  local copies, waits for them, and re-layouts  3.91 us (4%)
    pallas_call x1, Pallas kernels, per_device(): pl.pallas_call(functools.partial(kernel, (n_nodes, n_mp, chunks)), out_sh...  86.9 us
    unnamed x5, local copies, waits for them, and re-layouts  3.91 us

profile of v3, /device:TPU:11, one launch (start us, length us, event | category | flops | bytes accessed | tf_op | source)
XLA Modules:
  0.0 91.4 jit_solution(3575800635489606907)
XLA Ops:
  0.6 1.3 %copy.13.dec_ref = s32[8,2]{1,0:T(8,128)} copy(s32[8,2]{0,1:T(2,128)} %param.20) | data formatting | bytes 128 | tf_op args[9]
  2.0 86.9 %shard_map.122 = (bf16[1024,256]{1,0:T(8,128)(2,1)}, bf16[256,256]{1,0:T(8,128)(2,1)}) custom-call(s32[2,4]{1,0:T(2,128)} %enc_ref.1, s32[2,3]{1,0:T(2,128)} %proc_ref.1, s32[8,2]{1,0:T(8,128)} %copy.13.dec_ref, s32[64]{0:T(128)} %count_ref.1, bf16[1024,256]{1,0:T(8,128)(2,1)} %grid_ref.1, bf16[256,256]{1,0:T(8,128)(2,1)} %mesh_ref.1, ...), custom_call_target="tpu_custom_call" | custom-call | tf_op jit(solution)/shard_map/pallas_call | solution.py:484
  88.9 0.0 copy-start
  88.9 1.9 %copy.16 = bf16[1024,256]{1,0:T(8,128)(2,1)} copy(bf16[1024,256]{1,0:T(8,128)(2,1)} %get-tuple-element.4) | data formatting | bytes 1048576
  90.8 0.0 copy-done
  90.8 0.7 copy.17
Async XLA Ops:
  88.9 1.9 %copy-start = (bf16[256,256]{1,0:T(8,128)(2,1)S(1)}, bf16[256,256]{1,0:T(8,128)(2,1)}, u32[]{:S(2)}) copy-start(bf16[256,256]{1,0:T(8,128)(2,1)} %get-tuple-element.5) | copy-start | bytes 393220
